TPU v7x, 32 devices: a whole 2x2x4 slice. The times are simulated.
32 devices in a mesh: slab: 8 (over z, y), mem: 4 (over x, core).
Axes of the slice: x: 2, y: 2, z: 4, core: 2. Of those that a mesh axis runs over, the one named last changes fastest.
Arguments:
- starting_states_set: float32 [128, 64, 1024], P('mem', 'slab'), may hold values from -6 to 6
- land_mask: int32 [64, 1024], P('slab'), may hold values 0 or 1
- cell_class: int32 [64, 1024], P('slab'), may hold values from 0 to 7
- kappa_table: float32 [8], replicated, may hold values from 0.08 to 0.2
- flow_table: float32 [2, 8], replicated, may hold values from -0.3 to 0.3
- obs_index: int32 [1024], P('slab'), may hold values from 0 to 8191
- obs_values: float32 [1024], P('slab'), may hold values from -24 to 24
- obs_var: float32 [1024], P('slab'), may hold values from 0.1 to 1
Outputs:
- analysis: float32 [128, 64, 1024], P('mem', 'slab')
All inputs are finite; a program needn't handle non-finite values. No bound on the sum of `land_mask` on one device may be relied on, other than what follows from the above.
Results may differ from a plain program's by a relative error of at most 0.00016.
Values sent between devices are 32-bit elements; how exact they have to be, the bound alone decides.
A program may use at most 64 MiB of HBM per device.

v0:
```python
import jax
import jax.numpy as jnp
from jax import lax
from jax.sharding import PartitionSpec as P

STEPS = 8
ROOT_ITERATIONS = 8
NCLS = 8


def extended(block, sides, width):
    for axis, dim in sides:
        count = lax.axis_size(axis)
        forward = [(i, i + 1) for i in range(count - 1)]
        backward = [(target, source) for source, target in forward]
        low = lax.ppermute(
            lax.slice_in_dim(block, block.shape[dim] - width, None, axis=dim), axis, forward
        )
        high = lax.ppermute(lax.slice_in_dim(block, 0, width, axis=dim), axis, backward)
        block = jnp.concatenate([low, block, high], axis=dim)
    return block


def advance(center, north, south, diffusion, flow_east, flow_north, wet_cells):
    edge = jnp.zeros_like(center[..., :1])
    east = jnp.concatenate([center[..., 1:], edge], axis=-1)
    west = jnp.concatenate([edge, center[..., :-1]], axis=-1)
    spread = north + south + east + west - 4.0 * center
    return wet_cells * (
        center
        + diffusion * spread
        - 0.5 * flow_east * (east - west)
        - 0.5 * flow_north * (north - south)
    )


def coefficients(classes, mask_rows, kappa_table, flow_table):
    diffusion = jnp.zeros(classes.shape, jnp.float32)
    flow_east = jnp.zeros(classes.shape, jnp.float32)
    flow_north = jnp.zeros(classes.shape, jnp.float32)
    for label in range(NCLS):
        hit = classes == label
        diffusion = diffusion + jnp.where(hit, kappa_table[label], 0.0)
        flow_east = flow_east + jnp.where(hit, flow_table[0, label], 0.0)
        flow_north = flow_north + jnp.where(hit, flow_table[1, label], 0.0)
    return (diffusion, flow_east, flow_north, mask_rows.astype(jnp.float32))


def statistics(observed, values, variances, factor, ens_total):
    highest = lax.Precision.HIGHEST
    ybar = jnp.sum(observed, axis=0) / ens_total
    err = variances * factor
    anom = (observed - ybar) / jnp.sqrt(err * (ens_total - 1.0))
    dev = (values - ybar) / jnp.sqrt(err)
    return (jnp.dot(anom, anom.T, precision=highest), jnp.dot(anom, dev, precision=highest))


def local(
    starting_states_set,
    land_mask,
    cell_class,
    kappa_table,
    flow_table,
    obs_index,
    obs_values,
    obs_var,
):
    highest = lax.Precision.HIGHEST
    kd = starting_states_set.shape[0]
    rows = starting_states_set.shape[1]
    ens_total = kd * lax.axis_size("mem")
    current_profile = starting_states_set
    diffusion, flow_east, flow_north, wet_cells = coefficients(
        cell_class, land_mask, kappa_table, flow_table
    )
    for step in range(STEPS):
        padded = extended(current_profile, (("slab", 1),), 1)
        current_profile = advance(
            padded[:, 1:-1],
            padded[:, 2:],
            padded[:, :-2],
            diffusion,
            flow_east,
            flow_north,
            wet_cells,
        )
    raveled_vector = current_profile.reshape(kd, rows * current_profile.shape[2])
    observed = jnp.take(raveled_vector, obs_index, axis=1)
    slab_here = lax.axis_index("slab").astype(jnp.float32)
    factor = 1.0 + 2.0 * slab_here / float(lax.axis_size("slab") - 1)
    member_group = lax.axis_index("mem")
    columns = lax.all_to_all(observed, "mem", split_axis=1, concat_axis=0, tiled=True)
    count = columns.shape[1]
    values = lax.dynamic_slice_in_dim(obs_values, member_group * count, count)
    variances = lax.dynamic_slice_in_dim(obs_var, member_group * count, count)
    gram_part, proj_part = statistics(columns, values, variances, factor, ens_total)
    gram, proj = lax.psum((gram_part, proj_part), ("slab", "mem"))
    ident = jnp.eye(ens_total, dtype=jnp.float32)
    matrix = ident + gram
    scale = jnp.trace(matrix)
    upper = matrix / scale
    lower = ident
    for turn in range(ROOT_ITERATIONS):
        factor_q = 1.5 * ident - 0.5 * jnp.dot(lower, upper, precision=highest)
        upper = jnp.dot(upper, factor_q, precision=highest)
        lower = jnp.dot(factor_q, lower, precision=highest)
    transform_weights = lower / jnp.sqrt(scale)
    mean_w = jnp.dot(lower, jnp.dot(lower, proj, precision=highest), precision=highest) / (
        scale * jnp.sqrt(ens_total - 1.0)
    )
    total_w = transform_weights + mean_w[:, None]
    omega = 1.0 / ens_total + total_w - (jnp.sum(total_w, axis=0) / ens_total)[None, :]
    mixed = jnp.einsum(
        "ij,irc->jrc",
        omega,
        lax.all_to_all(current_profile, "mem", split_axis=2, concat_axis=0, tiled=True),
        precision=highest,
    )
    return lax.all_to_all(mixed, "mem", split_axis=0, concat_axis=2, tiled=True)


def solution(mesh):
    return jax.shard_map(
        local,
        mesh=mesh,
        in_specs=(
            P("mem", "slab", None),
            P("slab", None),
            P("slab", None),
            P(),
            P(),
            P("slab"),
            P("slab"),
            P("slab"),
        ),
        out_specs=P("mem", "slab", None),
        check_vma=False,
    )
```

profile of v0, /device:TPU:0, one launch (start us, length us, event | category | flops | bytes accessed | tf_op | source)
XLA Modules:
  0.0 308.6 jit_solution(16976725727790895447)
XLA Ops:
  6.5 1.9 copy.42
  8.4 0.7 fusion.44
  9.2 1.3 collective-permute-start
  10.5 5.5 %collective-permute-start.1 = (f32[32,1,1024]{2,0,1:T(8,128)}, f32[32,1,1024]{2,0,1:T(8,128)S(1)}, u32[]{:S(2)}, u32[]{:S(2)}) collective-permute-start(f32[32,1,1024]{2,0,1:T(8,128)} %get-tuple-element.42), channel_id=1, source_target_pairs={{0,4},{4,8},{8,12},{12,16},{16,20},{20,24},{24,28},{1,5},{5,9},{9,... | collective-permute-start | bytes 393224 | tf_op jit(solution)/shard_map/ppermute | solution.py:16
  16.4 0.7 fusion.47
  17.0 0.7 fusion.46
  17.8 5.0 %select_add_fusion = (f32[8,1024]{1,0:T(8,128)S(1)}, pred[8,1024]{1,0:T(8,128)(4,1)S(1)}, pred[8,1024]{1,0:T(8,128)(4,1)S(1)}, pred[8,1024]{1,0:T(8,128)(4,1)S(1...) fusion(f32[]{:T(128)} %bitcast.7, f32[]{:T(128)} %bitcast.6, ...), kind=kLoop, calls=%fused_computation.61 | loop fusion | flops 188416 | bytes 131104 | tf_op jit(solution)/shard_map/add | solution.py:43
  22.8 5.0 %add_multiply_fusion = f32[8,1024]{1,0:T(8,128)S(1)} fusion(pred[8,1024]{1,0:T(8,128)(4,1)S(1)} %get-tuple-element.13, pred[8,1024]{1,0:T(8,128)(4,1)S(1)} %get-tuple-element.12, pred[8,1024]{1,0:T(8,128)(4,1)S(1)} %get-tuple-element.11, pred[8,1024]{1,0:T(8,128)(4,1)S(1)} %get-tuple-element.10, pred[8,1024]{1,0:T(8,128)(4,1)S(1)} %get-tuple-element.9, ...), kind=kLoop, calls=%fused_computation.59 | loop fusion | flops 131072 | bytes 98336 | tf_op jit(solution)/shard_map/mul | solution.py:33
  27.8 5.0 %add_multiply_fusion.1 = f32[8,1024]{1,0:T(8,128)S(1)} fusion(pred[8,1024]{1,0:T(8,128)(4,1)S(1)} %get-tuple-element.13, pred[8,1024]{1,0:T(8,128)(4,1)S(1)} %get-tuple-element.12, pred[8,1024]{1,0:T(8,128)(4,1)S(1)} %get-tuple-element.11, pred[8,1024]{1,0:T(8,128)(4,1)S(1)} %get-tuple-element.10, pred[8,1024]{1,0:T(8,128)(4,1)S(1)} %get-tuple-element.9, ...), kind=kLoop, calls=%fused_computation.60 | loop fusion | flops 131072 | bytes 98336 | tf_op jit(solution)/shard_map/mul | solution.py:32
  33.0 0.6 subtract_multiply_fusion.7
  33.7 1.3 collective-permute-start.2
  35.0 5.4 %collective-permute-start.3 = (f32[32,1,1024]{2,0,1:T(8,128)S(1)}, f32[32,1,1024]{2,0,1:T(8,128)S(1)}, u32[]{:S(2)}, u32[]{:S(2)}) collective-permute-start(f32[32,1,1024]{2,0,1:T(8,128)S(1)} %get-tuple-element.38), channel_id=1, source_target_pairs={{0,4},{4,8},{8,12},{12,16},{16,20},{20,24},{24,28},{1,5},{5,9},{9,... | collective-permute-start | bytes 393224 | tf_op jit(solution)/shard_map/ppermute | solution.py:16
  41.4 2.9 collective-permute-done.3
  44.4 0.7 subtract_multiply_fusion.6
  45.1 1.3 collective-permute-start.4
  46.4 5.0 %collective-permute-start.5 = (f32[32,1,1024]{2,0,1:T(8,128)S(1)}, f32[32,1,1024]{2,0,1:T(8,128)S(1)}, u32[]{:S(2)}, u32[]{:S(2)}) collective-permute-start(f32[32,1,1024]{2,0,1:T(8,128)S(1)} %get-tuple-element.34), channel_id=1, source_target_pairs={{0,4},{4,8},{8,12},{12,16},{16,20},{20,24},{24,28},{1,5},{5,9},{9,... | collective-permute-start | bytes 393224 | tf_op jit(solution)/shard_map/ppermute | solution.py:16
  51.8 1.1 collective-permute-done.4
  52.9 3.0 collective-permute-done.5
  55.8 0.7 subtract_multiply_fusion.5
  56.5 1.3 collective-permute-start.6
  57.8 5.0 %collective-permute-start.7 = (f32[32,1,1024]{2,0,1:T(8,128)S(1)}, f32[32,1,1024]{2,0,1:T(8,128)S(1)}, u32[]{:S(2)}, u32[]{:S(2)}) collective-permute-start(f32[32,1,1024]{2,0,1:T(8,128)S(1)} %get-tuple-element.30), channel_id=1, source_target_pairs={{0,4},{4,8},{8,12},{12,16},{16,20},{20,24},{24,28},{1,5},{5,9},{9,... | collective-permute-start | bytes 393224 | tf_op jit(solution)/shard_map/ppermute | solution.py:16
  63.3 1.3 collective-permute-done.6
  64.6 3.0 collective-permute-done.7
  67.5 0.7 subtract_multiply_fusion.4
  68.2 1.3 collective-permute-start.8
  69.5 5.0 %collective-permute-start.9 = (f32[32,1,1024]{2,0,1:T(8,128)S(1)}, f32[32,1,1024]{2,0,1:T(8,128)S(1)}, u32[]{:S(2)}, u32[]{:S(2)}) collective-permute-start(f32[32,1,1024]{2,0,1:T(8,128)S(1)} %get-tuple-element.26), channel_id=1, source_target_pairs={{0,4},{4,8},{8,12},{12,16},{16,20},{20,24},{24,28},{1,5},{5,9},{9,... | collective-permute-start | bytes 393224 | tf_op jit(solution)/shard_map/ppermute | solution.py:16
  75.0 1.3 collective-permute-done.8
  76.3 3.0 collective-permute-done.9
  79.3 0.7 subtract_multiply_fusion.3
  80.0 1.3 collective-permute-start.10
  81.3 5.0 %collective-permute-start.11 = (f32[32,1,1024]{2,0,1:T(8,128)S(1)}, f32[32,1,1024]{2,0,1:T(8,128)S(1)}, u32[]{:S(2)}, u32[]{:S(2)}) collective-permute-start(f32[32,1,1024]{2,0,1:T(8,128)S(1)} %get-tuple-element.22), channel_id=1, source_target_pairs={{0,4},{4,8},{8,12},{12,16},{16,20},{20,24},{24,28},{1,5},{5,9},{9,... | collective-permute-start | bytes 393224 | tf_op jit(solution)/shard_map/ppermute | solution.py:16
  86.7 1.3 collective-permute-done.10
  88.0 3.0 collective-permute-done.11
  91.0 0.7 subtract_multiply_fusion.2
  91.7 1.3 collective-permute-start.12
  93.0 5.0 %collective-permute-start.13 = (f32[32,1,1024]{2,0,1:T(8,128)S(1)}, f32[32,1,1024]{2,0,1:T(8,128)S(1)}, u32[]{:S(2)}, u32[]{:S(2)}) collective-permute-start(f32[32,1,1024]{2,0,1:T(8,128)S(1)} %get-tuple-element.18), channel_id=1, source_target_pairs={{0,4},{4,8},{8,12},{12,16},{16,20},{20,24},{24,28},{1,5},{5,9},{9,... | collective-permute-start | bytes 393224 | tf_op jit(solution)/shard_map/ppermute | solution.py:16
  98.4 1.3 collective-permute-done.12
  99.7 3.0 collective-permute-done.13
  102.7 0.7 subtract_multiply_fusion.1
  103.4 1.3 collective-permute-start.14
  104.7 5.0 %collective-permute-start.15 = (f32[32,1,1024]{2,0,1:T(8,128)S(1)}, f32[32,1,1024]{2,0,1:T(8,128)S(1)}, u32[]{:S(2)}, u32[]{:S(2)}) collective-permute-start(f32[32,1,1024]{2,0,1:T(8,128)S(1)} %get-tuple-element.14), channel_id=1, source_target_pairs={{0,4},{4,8},{8,12},{12,16},{16,20},{20,24},{24,28},{1,5},{5,9},{9,... | collective-permute-start | bytes 393224 | tf_op jit(solution)/shard_map/ppermute | solution.py:16
  110.1 1.3 collective-permute-done.14
  111.5 3.0 collective-permute-done.15
  114.4 0.7 subtract_multiply_fusion
  115.1 2.6 copy.43
  117.7 2.8 gather_fusion
  120.7 0.7 reshape.69
  121.4 3.4 %all-to-all-start = ((f32[4,1,1024]{2,1,0:T(1,128)}), f32[4,1,1024]{2,1,0:T(1,128)S(1)}, u32[]{:S(2)}, u32[]{:S(2)}) async-start(f32[4,1,1024]{2,1,0:T(1,128)} %reshape.69), calls=%async_computation | async-start | bytes 32768 | tf_op jit(solution)/shard_map/all_to_all | solution.py:92
  124.9 2.7 copy.46
  127.6 4.8 %reshape.67 = f32[4,1,65536]{2,1,0:T(1,128)} reshape(f32[1024,8,32]{2,1,0:T(8,128)} %bitcast.117) | data formatting | bytes 2097152
  132.4 3.5 %all-to-all-start.1 = ((f32[4,1,65536]{2,1,0:T(1,128)}), f32[4,1,65536]{2,1,0:T(1,128)S(1)}, u32[]{:S(2)}, u32[]{:S(2)}) async-start(f32[4,1,65536]{2,1,0:T(1,128)} %reshape.67), calls=%async_computation.1 | async-start | bytes 2097152 | tf_op jit(solution)/shard_map/all_to_all | solution.py:116
  136.6 0.7 reduce.3
  137.9 0.9 fusion.49
  139.1 44.7 %psum.15 = f32[128]{0:T(128)S(1)} all-reduce(f32[128]{0:T(128)S(1)} %convolution_bitcast_fusion.2), channel_id=1, replica_groups=mesh['slab'=8,'mem'=4] {'slab','mem'}, use_global_device_ids=true, to_apply=%region_3.4 | all-reduce | flops 128 | bytes 1024 | tf_op jit(solution)/shard_map/psum | solution.py:97
  183.8 76.2 %all-reduce.18.cloned.1.call-done = f32[128,128]{1,0:T(8,128)} async-done(((f32[128,128]{1,0:T(8,128)}), f32[128,128]{1,0:T(8,128)}) %all-reduce.18.cloned.1.call-update) | async-done | bytes 65552 | tf_op jit(solution)/shard_map/psum | solution.py:97
  259.9 1.5 select_reduce_fusion
  261.4 1.6 fusion.7
  263.2 1.6 fusion.17
  270.8 3.7 %reduce.2 = f32[4,65536]{1,0:T(4,128)S(1)} reduce(f32[4,1,65536]{2,1,0:T(1,128)S(1)} %all-to-all-done.1, f32[]{:T(128)} %broadcast.130), dimensions={1}, to_apply=%all_to_all.41.reduce_sub_computation | reduce | bytes 2097156 | tf_op jit(solution)/shard_map/all_to_all | solution.py:116
  274.5 3.4 %reshape.68 = f32[1024,8,32]{2,1,0:T(8,128)} reshape(f32[4,65536]{1,0:T(4,128)S(1)} %reduce.2) | data formatting | bytes 2097152
  277.9 2.8 copy.47
  280.7 1.1 fusion.9
  282.4 18.2 %all_to_all.52 = f32[128,8,256]{2,1,0:T(8,128)S(1)} all-to-all(f32[128,8,256]{2,1,0:T(8,128)S(1)} %copy.49), channel_id=1, replica_groups=mesh['slab'=8,'mem'=4] {'mem'}, dimensions={0} | all-to-all | bytes 2097152 | tf_op jit(solution)/shard_map/all_to_all | solution.py:119
  300.6 1.1 copy.50
  (80 shorter events, 11.0 us)
Async XLA Ops:
  6.5 9.8 %copy-start.2 = (f32[8]{0:T(128)S(1)}, f32[8]{0:T(128)}, u32[]{:S(2)}) copy-start(f32[8]{0:T(128)} %param.11) | copy-start | bytes 100
  6.5 10.5 %copy-start = (f32[2,8]{1,0:T(2,128)S(1)}, f32[2,8]{1,0:T(2,128)}, u32[]{:S(2)}) copy-start(f32[2,8]{1,0:T(2,128)} %param.12) | copy-start | bytes 196
  6.5 11.2 %copy-start.5 = (s32[128]{0:T(128)S(1)}, s32[128]{0:T(128)}, u32[]{:S(2)}) copy-start(s32[128]{0:T(128)} %param.13) | copy-start | bytes 1540
  6.5 11.2 %copy-start.3 = (s32[8,1024]{1,0:T(8,128)S(1)}, s32[8,1024]{1,0:T(8,128)}, u32[]{:S(2)}) copy-start(s32[8,1024]{1,0:T(8,128)} %param.10) | copy-start | bytes 98308
  6.5 26.3 %copy-start.1 = (s32[8,1024]{1,0:T(8,128)S(1)}, s32[8,1024]{1,0:T(8,128)}, u32[]{:S(2)}) copy-start(s32[8,1024]{1,0:T(8,128)} %param.9) | copy-start | bytes 98308
  9.2 23.8 %collective-permute-start = (f32[32,1,1024]{2,0,1:T(8,128)}, f32[32,1,1024]{2,0,1:T(8,128)S(1)}, u32[]{:S(2)}, u32[]{:S(2)}) collective-permute-start(f32[32,1,1024]{2,0,1:T(8,128)} %get-tuple-element.43), channel_id=1, source_target_pairs={{4,0},{8,4},{12,8},{16,12},{20,16},{24,20},{28,24},{5,1},{9,5},{13... | collective-permute-start | bytes 393224 | tf_op jit(solution)/shard_map/ppermute | solution.py:19
  10.5 22.5 %collective-permute-start.1 = (f32[32,1,1024]{2,0,1:T(8,128)}, f32[32,1,1024]{2,0,1:T(8,128)S(1)}, u32[]{:S(2)}, u32[]{:S(2)}) collective-permute-start(f32[32,1,1024]{2,0,1:T(8,128)} %get-tuple-element.42), channel_id=1, source_target_pairs={{0,4},{4,8},{8,12},{12,16},{16,20},{20,24},{24,28},{1,5},{5,9},{9,... | collective-permute-start | bytes 393224 | tf_op jit(solution)/shard_map/ppermute | solution.py:16
  33.7 7.8 %collective-permute-start.2 = (f32[32,1,1024]{2,0,1:T(8,128)S(1)}, f32[32,1,1024]{2,0,1:T(8,128)S(1)}, u32[]{:S(2)}, u32[]{:S(2)}) collective-permute-start(f32[32,1,1024]{2,0,1:T(8,128)S(1)} %get-tuple-element.39), channel_id=1, source_target_pairs={{4,0},{8,4},{12,8},{16,12},{20,16},{24,20},{28,24},{5,1},{9,5},{13... | collective-permute-start | bytes 393224 | tf_op jit(solution)/shard_map/ppermute | solution.py:19
  35.0 9.4 %collective-permute-start.3 = (f32[32,1,1024]{2,0,1:T(8,128)S(1)}, f32[32,1,1024]{2,0,1:T(8,128)S(1)}, u32[]{:S(2)}, u32[]{:S(2)}) collective-permute-start(f32[32,1,1024]{2,0,1:T(8,128)S(1)} %get-tuple-element.38), channel_id=1, source_target_pairs={{0,4},{4,8},{8,12},{12,16},{16,20},{20,24},{24,28},{1,5},{5,9},{9,... | collective-permute-start | bytes 393224 | tf_op jit(solution)/shard_map/ppermute | solution.py:16
  45.1 7.8 %collective-permute-start.4 = (f32[32,1,1024]{2,0,1:T(8,128)S(1)}, f32[32,1,1024]{2,0,1:T(8,128)S(1)}, u32[]{:S(2)}, u32[]{:S(2)}) collective-permute-start(f32[32,1,1024]{2,0,1:T(8,128)S(1)} %get-tuple-element.35), channel_id=1, source_target_pairs={{4,0},{8,4},{12,8},{16,12},{20,16},{24,20},{28,24},{5,1},{9,5},{13... | collective-permute-start | bytes 393224 | tf_op jit(solution)/shard_map/ppermute | solution.py:19
  46.4 9.5 %collective-permute-start.5 = (f32[32,1,1024]{2,0,1:T(8,128)S(1)}, f32[32,1,1024]{2,0,1:T(8,128)S(1)}, u32[]{:S(2)}, u32[]{:S(2)}) collective-permute-start(f32[32,1,1024]{2,0,1:T(8,128)S(1)} %get-tuple-element.34), channel_id=1, source_target_pairs={{0,4},{4,8},{8,12},{12,16},{16,20},{20,24},{24,28},{1,5},{5,9},{9,... | collective-permute-start | bytes 393224 | tf_op jit(solution)/shard_map/ppermute | solution.py:16
  56.5 8.1 %collective-permute-start.6 = (f32[32,1,1024]{2,0,1:T(8,128)S(1)}, f32[32,1,1024]{2,0,1:T(8,128)S(1)}, u32[]{:S(2)}, u32[]{:S(2)}) collective-permute-start(f32[32,1,1024]{2,0,1:T(8,128)S(1)} %get-tuple-element.31), channel_id=1, source_target_pairs={{4,0},{8,4},{12,8},{16,12},{20,16},{24,20},{28,24},{5,1},{9,5},{13... | collective-permute-start | bytes 393224 | tf_op jit(solution)/shard_map/ppermute | solution.py:19
  57.8 9.7 %collective-permute-start.7 = (f32[32,1,1024]{2,0,1:T(8,128)S(1)}, f32[32,1,1024]{2,0,1:T(8,128)S(1)}, u32[]{:S(2)}, u32[]{:S(2)}) collective-permute-start(f32[32,1,1024]{2,0,1:T(8,128)S(1)} %get-tuple-element.30), channel_id=1, source_target_pairs={{0,4},{4,8},{8,12},{12,16},{16,20},{20,24},{24,28},{1,5},{5,9},{9,... | collective-permute-start | bytes 393224 | tf_op jit(solution)/shard_map/ppermute | solution.py:16
  68.2 8.1 %collective-permute-start.8 = (f32[32,1,1024]{2,0,1:T(8,128)S(1)}, f32[32,1,1024]{2,0,1:T(8,128)S(1)}, u32[]{:S(2)}, u32[]{:S(2)}) collective-permute-start(f32[32,1,1024]{2,0,1:T(8,128)S(1)} %get-tuple-element.27), channel_id=1, source_target_pairs={{4,0},{8,4},{12,8},{16,12},{20,16},{24,20},{28,24},{5,1},{9,5},{13... | collective-permute-start | bytes 393224 | tf_op jit(solution)/shard_map/ppermute | solution.py:19
  69.5 9.7 %collective-permute-start.9 = (f32[32,1,1024]{2,0,1:T(8,128)S(1)}, f32[32,1,1024]{2,0,1:T(8,128)S(1)}, u32[]{:S(2)}, u32[]{:S(2)}) collective-permute-start(f32[32,1,1024]{2,0,1:T(8,128)S(1)} %get-tuple-element.26), channel_id=1, source_target_pairs={{0,4},{4,8},{8,12},{12,16},{16,20},{20,24},{24,28},{1,5},{5,9},{9,... | collective-permute-start | bytes 393224 | tf_op jit(solution)/shard_map/ppermute | solution.py:16
  80.0 8.1 %collective-permute-start.10 = (f32[32,1,1024]{2,0,1:T(8,128)S(1)}, f32[32,1,1024]{2,0,1:T(8,128)S(1)}, u32[]{:S(2)}, u32[]{:S(2)}) collective-permute-start(f32[32,1,1024]{2,0,1:T(8,128)S(1)} %get-tuple-element.23), channel_id=1, source_target_pairs={{4,0},{8,4},{12,8},{16,12},{20,16},{24,20},{28,24},{5,1},{9,5},{13... | collective-permute-start | bytes 393224 | tf_op jit(solution)/shard_map/ppermute | solution.py:19
  81.3 9.7 %collective-permute-start.11 = (f32[32,1,1024]{2,0,1:T(8,128)S(1)}, f32[32,1,1024]{2,0,1:T(8,128)S(1)}, u32[]{:S(2)}, u32[]{:S(2)}) collective-permute-start(f32[32,1,1024]{2,0,1:T(8,128)S(1)} %get-tuple-element.22), channel_id=1, source_target_pairs={{0,4},{4,8},{8,12},{12,16},{16,20},{20,24},{24,28},{1,5},{5,9},{9,... | collective-permute-start | bytes 393224 | tf_op jit(solution)/shard_map/ppermute | solution.py:16
  91.7 8.1 %collective-permute-start.12 = (f32[32,1,1024]{2,0,1:T(8,128)S(1)}, f32[32,1,1024]{2,0,1:T(8,128)S(1)}, u32[]{:S(2)}, u32[]{:S(2)}) collective-permute-start(f32[32,1,1024]{2,0,1:T(8,128)S(1)} %get-tuple-element.19), channel_id=1, source_target_pairs={{4,0},{8,4},{12,8},{16,12},{20,16},{24,20},{28,24},{5,1},{9,5},{13... | collective-permute-start | bytes 393224 | tf_op jit(solution)/shard_map/ppermute | solution.py:19
  93.0 9.7 %collective-permute-start.13 = (f32[32,1,1024]{2,0,1:T(8,128)S(1)}, f32[32,1,1024]{2,0,1:T(8,128)S(1)}, u32[]{:S(2)}, u32[]{:S(2)}) collective-permute-start(f32[32,1,1024]{2,0,1:T(8,128)S(1)} %get-tuple-element.18), channel_id=1, source_target_pairs={{0,4},{4,8},{8,12},{12,16},{16,20},{20,24},{24,28},{1,5},{5,9},{9,... | collective-permute-start | bytes 393224 | tf_op jit(solution)/shard_map/ppermute | solution.py:16
  103.4 8.1 %collective-permute-start.14 = (f32[32,1,1024]{2,0,1:T(8,128)S(1)}, f32[32,1,1024]{2,0,1:T(8,128)S(1)}, u32[]{:S(2)}, u32[]{:S(2)}) collective-permute-start(f32[32,1,1024]{2,0,1:T(8,128)S(1)} %get-tuple-element.15), channel_id=1, source_target_pairs={{4,0},{8,4},{12,8},{16,12},{20,16},{24,20},{28,24},{5,1},{9,5},{13... | collective-permute-start | bytes 393224 | tf_op jit(solution)/shard_map/ppermute | solution.py:19
  104.7 9.7 %collective-permute-start.15 = (f32[32,1,1024]{2,0,1:T(8,128)S(1)}, f32[32,1,1024]{2,0,1:T(8,128)S(1)}, u32[]{:S(2)}, u32[]{:S(2)}) collective-permute-start(f32[32,1,1024]{2,0,1:T(8,128)S(1)} %get-tuple-element.14), channel_id=1, source_target_pairs={{0,4},{4,8},{8,12},{12,16},{16,20},{20,24},{24,28},{1,5},{5,9},{9,... | collective-permute-start | bytes 393224 | tf_op jit(solution)/shard_map/ppermute | solution.py:16
  114.4 10.4 %copy-start.4 = (f32[128]{0:T(128)S(1)}, f32[128]{0:T(128)}, u32[]{:S(2)}) copy-start(f32[128]{0:T(128)} %param.15) | copy-start | bytes 1540
  121.4 11.1 %all-to-all-start = ((f32[4,1,1024]{2,1,0:T(1,128)}), f32[4,1,1024]{2,1,0:T(1,128)S(1)}, u32[]{:S(2)}, u32[]{:S(2)}) async-start(f32[4,1,1024]{2,1,0:T(1,128)} %reshape.69), calls=%async_computation | async-start | bytes 32768 | tf_op jit(solution)/shard_map/all_to_all | solution.py:92
  127.6 11.3 %copy-start.6 = (f32[128]{0:T(128)S(1)}, f32[128]{0:T(128)}, u32[]{:S(2)}) copy-start(f32[128]{0:T(128)} %param.14) | copy-start | bytes 1540
  132.4 138.3 %all-to-all-start.1 = ((f32[4,1,65536]{2,1,0:T(1,128)}), f32[4,1,65536]{2,1,0:T(1,128)S(1)}, u32[]{:S(2)}, u32[]{:S(2)}) async-start(f32[4,1,65536]{2,1,0:T(1,128)} %reshape.67), calls=%async_computation.1 | async-start | bytes 2097152 | tf_op jit(solution)/shard_map/all_to_all | solution.py:116
  136.0 124.0 %all-reduce.18.cloned.1.call-start = ((), (), s32[]{:S(2)}) async-start(), calls=%async_computation.3 | async-start | bytes 131072 | tf_op jit(solution)/shard_map/psum | solution.py:97
Sparse Core Ops, SparseCore 0:
  142.4 117.4 all-reduce.17
where the time goes:
time: 310 us; the launch traced here: 309 us
  waiting for transfers between devices  105 us (34%)
  blocking collectives  62.9 us (20%)
  starting transfers between devices  58.4 us (19%)
  local copies, waits for them, and re-layouts  29.9 us (10%)
  other arithmetic  26.7 us (9%)
  between operations  15.3 us (5%)
  matrix products  10.1 us (3%)
    psum x1, waiting for transfers between devices, local(): gram, proj = lax.psum((gram_part, proj_part), ('slab', 'mem'))  76.2 us
    psum x1, blocking collectives, local(): gram, proj = lax.psum((gram_part, proj_part), ('slab', 'mem'))  44.7 us
    ppermute x8, starting transfers between devices, extended(): lax.ppermute(lax.slice_in_dim(block, block.shape[dim] - width, None, axis...  41.1 us
    ppermute x8, waiting for transfers between devices, extended(): lax.ppermute(lax.slice_in_dim(block, block.shape[dim] - width, None, axis...  20.7 us
    all_to_all x1, blocking collectives, local(): return lax.all_to_all(mixed, 'mem', split_axis=0, concat_axis=2, tiled=True)  18.2 us
    unnamed x19, local copies, waits for them, and re-layouts  10.9 us
    ppermute x8, starting transfers between devices, extended(): lax.ppermute(lax.slice_in_dim(block, 0, width, axis=dim), axis, backward)  10.3 us
    ppermute x8, waiting for transfers between devices, extended(): lax.ppermute(lax.slice_in_dim(block, 0, width, axis=dim), axis, backward)  8.4 us
  transfers between devices with their start and end apart: 19, of which 15 were waited for; matrix products, arithmetic and copies ran while one was open for 13% of the time, Pallas kernels for 0%

commit v1 on v0

--- a/solution.py
+++ b/solution.py
@@ -94,7 +94,7 @@
     values = lax.dynamic_slice_in_dim(obs_values, member_group * count, count)
     variances = lax.dynamic_slice_in_dim(obs_var, member_group * count, count)
     gram_part, proj_part = statistics(columns, values, variances, factor, ens_total)
-    gram, proj = lax.psum((gram_part, proj_part), ("slab", "mem"))
+    gram, proj = lax.psum(lax.psum((gram_part, proj_part), "mem"), "slab")
     ident = jnp.eye(ens_total, dtype=jnp.float32)
     matrix = ident + gram
     scale = jnp.trace(matrix)

time: 310 us -> 292 us (0.942)
  blocking collectives: 62.9 us -> 44.2 us
    psum x1 -> x2, blocking collectives: 44.7 us -> 27.2 us  [local(): gram, proj = lax.psum(lax.psum((gram_part, proj_part), 'mem'), 'slab')]
    psum x1 -> x2, waiting for transfers between devices: 76.2 us -> 76.3 us  [local(): gram, proj = lax.psum(lax.psum((gram_part, proj_part), 'mem'), 'slab')]
  transfers between devices with their start and end apart: 19 -> 20, of which waited for: 15 -> 16; matrix products, arithmetic and copies ran while one was open for 13% -> 14% of each run, Pallas kernels for 0% -> 0%
where the time goes in v1:
time: 292 us; the launch traced here: 290 us
  waiting for transfers between devices  105 us (36%)
  starting transfers between devices  58.4 us (20%)
  blocking collectives  44.2 us (15%)
  local copies, waits for them, and re-layouts  29.9 us (10%)
  other arithmetic  26.6 us (9%)
  between operations  15.5 us (5%)
  matrix products  10.3 us (4%)
    psum x2, waiting for transfers between devices, local(): gram, proj = lax.psum(lax.psum((gram_part, proj_part), 'mem'), 'slab')  76.3 us
    ppermute x8, starting transfers between devices, extended(): lax.ppermute(lax.slice_in_dim(block, block.shape[dim] - width, None, axis...  41.1 us
    psum x2, blocking collectives, local(): gram, proj = lax.psum(lax.psum((gram_part, proj_part), 'mem'), 'slab')  27.2 us
    ppermute x8, waiting for transfers between devices, extended(): lax.ppermute(lax.slice_in_dim(block, block.shape[dim] - width, None, axis...  20.7 us
    all_to_all x1, blocking collectives, local(): return lax.all_to_all(mixed, 'mem', split_axis=0, concat_axis=2, tiled=True)  17 us
    unnamed x19, local copies, waits for them, and re-layouts  10.9 us
    ppermute x8, starting transfers between devices, extended(): lax.ppermute(lax.slice_in_dim(block, 0, width, axis=dim), axis, backward)  10.3 us
    ppermute x8, waiting for transfers between devices, extended(): lax.ppermute(lax.slice_in_dim(block, 0, width, axis=dim), axis, backward)  8.4 us
  transfers between devices with their start and end apart: 20, of which 16 were waited for; matrix products, arithmetic and copies ran while one was open for 14% of the time, Pallas kernels for 0%

profile of v1, /device:TPU:0, one launch (start us, length us, event | category | flops | bytes accessed | tf_op | source)
XLA Modules:
  0.0 290.4 jit_solution(12560306184917314220)
XLA Ops:
  6.5 1.9 copy.42
  8.4 0.7 fusion.44
  9.1 1.3 collective-permute-start
  10.4 5.5 %collective-permute-start.1 = (f32[32,1,1024]{2,0,1:T(8,128)}, f32[32,1,1024]{2,0,1:T(8,128)S(1)}, u32[]{:S(2)}, u32[]{:S(2)}) collective-permute-start(f32[32,1,1024]{2,0,1:T(8,128)} %get-tuple-element.42), channel_id=1, source_target_pairs={{0,4},{4,8},{8,12},{12,16},{16,20},{20,24},{24,28},{1,5},{5,9},{9,... | collective-permute-start | bytes 393224 | tf_op jit(solution)/shard_map/ppermute | solution.py:16
  16.3 0.7 fusion.47
  17.0 0.7 fusion.46
  17.7 5.0 %select_add_fusion = (f32[8,1024]{1,0:T(8,128)S(1)}, pred[8,1024]{1,0:T(8,128)(4,1)S(1)}, pred[8,1024]{1,0:T(8,128)(4,1)S(1)}, pred[8,1024]{1,0:T(8,128)(4,1)S(1...) fusion(f32[]{:T(128)} %bitcast.7, f32[]{:T(128)} %bitcast.6, ...), kind=kLoop, calls=%fused_computation.61 | loop fusion | flops 188416 | bytes 131104 | tf_op jit(solution)/shard_map/add | solution.py:43
  22.8 5.0 %add_multiply_fusion = f32[8,1024]{1,0:T(8,128)S(1)} fusion(pred[8,1024]{1,0:T(8,128)(4,1)S(1)} %get-tuple-element.13, pred[8,1024]{1,0:T(8,128)(4,1)S(1)} %get-tuple-element.12, pred[8,1024]{1,0:T(8,128)(4,1)S(1)} %get-tuple-element.11, pred[8,1024]{1,0:T(8,128)(4,1)S(1)} %get-tuple-element.10, pred[8,1024]{1,0:T(8,128)(4,1)S(1)} %get-tuple-element.9, ...), kind=kLoop, calls=%fused_computation.59 | loop fusion | flops 131072 | bytes 98336 | tf_op jit(solution)/shard_map/mul | solution.py:33
  27.7 5.0 %add_multiply_fusion.1 = f32[8,1024]{1,0:T(8,128)S(1)} fusion(pred[8,1024]{1,0:T(8,128)(4,1)S(1)} %get-tuple-element.13, pred[8,1024]{1,0:T(8,128)(4,1)S(1)} %get-tuple-element.12, pred[8,1024]{1,0:T(8,128)(4,1)S(1)} %get-tuple-element.11, pred[8,1024]{1,0:T(8,128)(4,1)S(1)} %get-tuple-element.10, pred[8,1024]{1,0:T(8,128)(4,1)S(1)} %get-tuple-element.9, ...), kind=kLoop, calls=%fused_computation.60 | loop fusion | flops 131072 | bytes 98336 | tf_op jit(solution)/shard_map/mul | solution.py:32
  33.5 1.3 collective-permute-start.2
  34.8 5.4 %collective-permute-start.3 = (f32[32,1,1024]{2,0,1:T(8,128)S(1)}, f32[32,1,1024]{2,0,1:T(8,128)S(1)}, u32[]{:S(2)}, u32[]{:S(2)}) collective-permute-start(f32[32,1,1024]{2,0,1:T(8,128)S(1)} %get-tuple-element.38), channel_id=1, source_target_pairs={{0,4},{4,8},{8,12},{12,16},{16,20},{20,24},{24,28},{1,5},{5,9},{9,... | collective-permute-start | bytes 393224 | tf_op jit(solution)/shard_map/ppermute | solution.py:16
  41.3 2.9 %collective-permute-done.3 = f32[32,1,1024]{2,0,1:T(8,128)S(1)} collective-permute-done((f32[32,1,1024]{2,0,1:T(8,128)S(1)}, f32[32,1,1024]{2,0,1:T(8,128)S(1)}, u32[]{:S(2)}, u32[]{:S(2)}) %collective-permute-start.3) | collective-permute-done | bytes 131104 | tf_op jit(solution)/shard_map/ppermute | solution.py:16
  44.2 0.7 subtract_multiply_fusion.6
  44.9 1.3 collective-permute-start.4
  46.2 5.0 %collective-permute-start.5 = (f32[32,1,1024]{2,0,1:T(8,128)S(1)}, f32[32,1,1024]{2,0,1:T(8,128)S(1)}, u32[]{:S(2)}, u32[]{:S(2)}) collective-permute-start(f32[32,1,1024]{2,0,1:T(8,128)S(1)} %get-tuple-element.34), channel_id=1, source_target_pairs={{0,4},{4,8},{8,12},{12,16},{16,20},{20,24},{24,28},{1,5},{5,9},{9,... | collective-permute-start | bytes 393224 | tf_op jit(solution)/shard_map/ppermute | solution.py:16
  51.6 1.1 collective-permute-done.4
  52.7 3.0 %collective-permute-done.5 = f32[32,1,1024]{2,0,1:T(8,128)S(1)} collective-permute-done((f32[32,1,1024]{2,0,1:T(8,128)S(1)}, f32[32,1,1024]{2,0,1:T(8,128)S(1)}, u32[]{:S(2)}, u32[]{:S(2)}) %collective-permute-start.5) | collective-permute-done | bytes 131104 | tf_op jit(solution)/shard_map/ppermute | solution.py:16
  56.4 1.3 collective-permute-start.6
  57.7 5.0 %collective-permute-start.7 = (f32[32,1,1024]{2,0,1:T(8,128)S(1)}, f32[32,1,1024]{2,0,1:T(8,128)S(1)}, u32[]{:S(2)}, u32[]{:S(2)}) collective-permute-start(f32[32,1,1024]{2,0,1:T(8,128)S(1)} %get-tuple-element.30), channel_id=1, source_target_pairs={{0,4},{4,8},{8,12},{12,16},{16,20},{20,24},{24,28},{1,5},{5,9},{9,... | collective-permute-start | bytes 393224 | tf_op jit(solution)/shard_map/ppermute | solution.py:16
  63.1 1.3 collective-permute-done.6
  64.4 3.0 %collective-permute-done.7 = f32[32,1,1024]{2,0,1:T(8,128)S(1)} collective-permute-done((f32[32,1,1024]{2,0,1:T(8,128)S(1)}, f32[32,1,1024]{2,0,1:T(8,128)S(1)}, u32[]{:S(2)}, u32[]{:S(2)}) %collective-permute-start.7) | collective-permute-done | bytes 131104 | tf_op jit(solution)/shard_map/ppermute | solution.py:16
  67.4 0.7 subtract_multiply_fusion.4
  68.1 1.3 collective-permute-start.8
  69.4 5.0 %collective-permute-start.9 = (f32[32,1,1024]{2,0,1:T(8,128)S(1)}, f32[32,1,1024]{2,0,1:T(8,128)S(1)}, u32[]{:S(2)}, u32[]{:S(2)}) collective-permute-start(f32[32,1,1024]{2,0,1:T(8,128)S(1)} %get-tuple-element.26), channel_id=1, source_target_pairs={{0,4},{4,8},{8,12},{12,16},{16,20},{20,24},{24,28},{1,5},{5,9},{9,... | collective-permute-start | bytes 393224 | tf_op jit(solution)/shard_map/ppermute | solution.py:16
  74.8 1.3 collective-permute-done.8
  76.2 3.0 %collective-permute-done.9 = f32[32,1,1024]{2,0,1:T(8,128)S(1)} collective-permute-done((f32[32,1,1024]{2,0,1:T(8,128)S(1)}, f32[32,1,1024]{2,0,1:T(8,128)S(1)}, u32[]{:S(2)}, u32[]{:S(2)}) %collective-permute-start.9) | collective-permute-done | bytes 131104 | tf_op jit(solution)/shard_map/ppermute | solution.py:16
  79.1 0.7 subtract_multiply_fusion.3
  79.8 1.3 collective-permute-start.10
  81.1 5.0 %collective-permute-start.11 = (f32[32,1,1024]{2,0,1:T(8,128)S(1)}, f32[32,1,1024]{2,0,1:T(8,128)S(1)}, u32[]{:S(2)}, u32[]{:S(2)}) collective-permute-start(f32[32,1,1024]{2,0,1:T(8,128)S(1)} %get-tuple-element.22), channel_id=1, source_target_pairs={{0,4},{4,8},{8,12},{12,16},{16,20},{20,24},{24,28},{1,5},{5,9},{9,... | collective-permute-start | bytes 393224 | tf_op jit(solution)/shard_map/ppermute | solution.py:16
  86.5 1.3 collective-permute-done.10
  87.9 3.0 %collective-permute-done.11 = f32[32,1,1024]{2,0,1:T(8,128)S(1)} collective-permute-done((f32[32,1,1024]{2,0,1:T(8,128)S(1)}, f32[32,1,1024]{2,0,1:T(8,128)S(1)}, u32[]{:S(2)}, u32[]{:S(2)}) %collective-permute-start.11) | collective-permute-done | bytes 131104 | tf_op jit(solution)/shard_map/ppermute | solution.py:16
  90.8 0.7 subtract_multiply_fusion.2
  91.5 1.3 collective-permute-start.12
  92.8 5.0 %collective-permute-start.13 = (f32[32,1,1024]{2,0,1:T(8,128)S(1)}, f32[32,1,1024]{2,0,1:T(8,128)S(1)}, u32[]{:S(2)}, u32[]{:S(2)}) collective-permute-start(f32[32,1,1024]{2,0,1:T(8,128)S(1)} %get-tuple-element.18), channel_id=1, source_target_pairs={{0,4},{4,8},{8,12},{12,16},{16,20},{20,24},{24,28},{1,5},{5,9},{9,... | collective-permute-start | bytes 393224 | tf_op jit(solution)/shard_map/ppermute | solution.py:16
  98.3 1.3 collective-permute-done.12
  99.6 3.0 %collective-permute-done.13 = f32[32,1,1024]{2,0,1:T(8,128)S(1)} collective-permute-done((f32[32,1,1024]{2,0,1:T(8,128)S(1)}, f32[32,1,1024]{2,0,1:T(8,128)S(1)}, u32[]{:S(2)}, u32[]{:S(2)}) %collective-permute-start.13) | collective-permute-done | bytes 131104 | tf_op jit(solution)/shard_map/ppermute | solution.py:16
  102.6 0.7 subtract_multiply_fusion.1
  103.3 1.3 collective-permute-start.14
  104.6 5.0 %collective-permute-start.15 = (f32[32,1,1024]{2,0,1:T(8,128)S(1)}, f32[32,1,1024]{2,0,1:T(8,128)S(1)}, u32[]{:S(2)}, u32[]{:S(2)}) collective-permute-start(f32[32,1,1024]{2,0,1:T(8,128)S(1)} %get-tuple-element.14), channel_id=1, source_target_pairs={{0,4},{4,8},{8,12},{12,16},{16,20},{20,24},{24,28},{1,5},{5,9},{9,... | collective-permute-start | bytes 393224 | tf_op jit(solution)/shard_map/ppermute | solution.py:16
  110.0 1.3 collective-permute-done.14
  111.3 3.0 %collective-permute-done.15 = f32[32,1,1024]{2,0,1:T(8,128)S(1)} collective-permute-done((f32[32,1,1024]{2,0,1:T(8,128)S(1)}, f32[32,1,1024]{2,0,1:T(8,128)S(1)}, u32[]{:S(2)}, u32[]{:S(2)}) %collective-permute-start.15) | collective-permute-done | bytes 131104 | tf_op jit(solution)/shard_map/ppermute | solution.py:16
  114.3 0.7 subtract_multiply_fusion
  115.0 2.6 copy.43
  117.6 2.8 gather_fusion
  120.5 0.7 reshape.69
  121.2 3.4 %all-to-all-start = ((f32[4,1,1024]{2,1,0:T(1,128)}), f32[4,1,1024]{2,1,0:T(1,128)S(1)}, u32[]{:S(2)}, u32[]{:S(2)}) async-start(f32[4,1,1024]{2,1,0:T(1,128)} %reshape.69), calls=%async_computation | async-start | bytes 32768 | tf_op jit(solution)/shard_map/all_to_all | solution.py:92
  124.7 2.7 copy.46
  127.4 4.8 %reshape.67 = f32[4,1,65536]{2,1,0:T(1,128)} reshape(f32[1024,8,32]{2,1,0:T(8,128)} %bitcast.117) | data formatting | bytes 2097152
  132.3 3.5 %all-to-all-start.1 = ((f32[4,1,65536]{2,1,0:T(1,128)}), f32[4,1,65536]{2,1,0:T(1,128)S(1)}, u32[]{:S(2)}, u32[]{:S(2)}) async-start(f32[4,1,65536]{2,1,0:T(1,128)} %reshape.67), calls=%async_computation.1 | async-start | bytes 2097152 | tf_op jit(solution)/shard_map/all_to_all | solution.py:116
  136.4 0.7 reduce.3
  137.6 0.9 fusion.49
  138.7 31.4 %all-reduce.19.cloned.1.call-done = f32[128,128]{1,0:T(8,128)} async-done(((f32[128,128]{1,0:T(8,128)}), f32[128,128]{1,0:T(8,128)}) %all-reduce.19.cloned.1.call-update) | async-done | bytes 65552 | tf_op jit(solution)/shard_map/psum | solution.py:97
  170.4 5.7 %psum.30 = f32[128]{0:T(128)S(1)} all-reduce(f32[128]{0:T(128)S(1)} %convolution_bitcast_fusion.2), channel_id=1, replica_groups=mesh['slab'=8,'mem'=4] {'mem'}, use_global_device_ids=true, to_apply=%region_4.5 | all-reduce | flops 128 | bytes 1024 | tf_op jit(solution)/shard_map/psum | solution.py:97
  176.1 21.5 %psum.31 = f32[128]{0:T(128)S(1)} all-reduce(f32[128]{0:T(128)S(1)} %psum.30), channel_id=1, replica_groups=mesh['slab'=8,'mem'=4] {'slab'}, use_global_device_ids=true, to_apply=%region_5.6 | all-reduce | flops 128 | bytes 1024 | tf_op jit(solution)/shard_map/psum | solution.py:97
  197.6 44.9 %all-reduce.21.cloned.1.call-done = f32[128,128]{1,0:T(8,128)} async-done(((f32[128,128]{1,0:T(8,128)}), f32[128,128]{1,0:T(8,128)}) %all-reduce.21.cloned.1.call-update) | async-done | bytes 65552 | tf_op jit(solution)/shard_map/psum | solution.py:97
  242.5 1.5 select_reduce_fusion
  244.0 1.7 fusion.7
  245.9 1.7 fusion.17
  253.9 3.7 %reduce.2 = f32[4,65536]{1,0:T(4,128)S(1)} reduce(f32[4,1,65536]{2,1,0:T(1,128)S(1)} %all-to-all-done.1, f32[]{:T(128)} %broadcast.130), dimensions={1}, to_apply=%all_to_all.41.reduce_sub_computation | reduce | bytes 2097156 | tf_op jit(solution)/shard_map/all_to_all | solution.py:116
  257.6 3.4 %reshape.68 = f32[1024,8,32]{2,1,0:T(8,128)} reshape(f32[4,65536]{1,0:T(4,128)S(1)} %reduce.2) | data formatting | bytes 2097152
  261.0 2.8 copy.47
  263.8 1.1 fusion.9
  265.5 17.0 %all_to_all.52 = f32[128,8,256]{2,1,0:T(8,128)S(1)} all-to-all(f32[128,8,256]{2,1,0:T(8,128)S(1)} %copy.49), channel_id=1, replica_groups=mesh['slab'=8,'mem'=4] {'mem'}, dimensions={0} | all-to-all | bytes 2097152 | tf_op jit(solution)/shard_map/all_to_all | solution.py:119
  282.5 1.1 copy.50
  (84 shorter events, 12.3 us)
Async XLA Ops:
  6.5 9.8 %copy-start.2 = (f32[8]{0:T(128)S(1)}, f32[8]{0:T(128)}, u32[]{:S(2)}) copy-start(f32[8]{0:T(128)} %param.11) | copy-start | bytes 100
  6.5 10.5 %copy-start = (f32[2,8]{1,0:T(2,128)S(1)}, f32[2,8]{1,0:T(2,128)}, u32[]{:S(2)}) copy-start(f32[2,8]{1,0:T(2,128)} %param.12) | copy-start | bytes 196
  6.5 11.2 %copy-start.5 = (s32[128]{0:T(128)S(1)}, s32[128]{0:T(128)}, u32[]{:S(2)}) copy-start(s32[128]{0:T(128)} %param.13) | copy-start | bytes 1540
  6.5 11.2 %copy-start.3 = (s32[8,1024]{1,0:T(8,128)S(1)}, s32[8,1024]{1,0:T(8,128)}, u32[]{:S(2)}) copy-start(s32[8,1024]{1,0:T(8,128)} %param.10) | copy-start | bytes 98308
  6.5 26.2 %copy-start.1 = (s32[8,1024]{1,0:T(8,128)S(1)}, s32[8,1024]{1,0:T(8,128)}, u32[]{:S(2)}) copy-start(s32[8,1024]{1,0:T(8,128)} %param.9) | copy-start | bytes 98308
  9.1 23.7 %collective-permute-start = (f32[32,1,1024]{2,0,1:T(8,128)}, f32[32,1,1024]{2,0,1:T(8,128)S(1)}, u32[]{:S(2)}, u32[]{:S(2)}) collective-permute-start(f32[32,1,1024]{2,0,1:T(8,128)} %get-tuple-element.43), channel_id=1, source_target_pairs={{4,0},{8,4},{12,8},{16,12},{20,16},{24,20},{28,24},{5,1},{9,5},{13... | collective-permute-start | bytes 393224 | tf_op jit(solution)/shard_map/ppermute | solution.py:19
  10.4 22.4 %collective-permute-start.1 = (f32[32,1,1024]{2,0,1:T(8,128)}, f32[32,1,1024]{2,0,1:T(8,128)S(1)}, u32[]{:S(2)}, u32[]{:S(2)}) collective-permute-start(f32[32,1,1024]{2,0,1:T(8,128)} %get-tuple-element.42), channel_id=1, source_target_pairs={{0,4},{4,8},{8,12},{12,16},{16,20},{20,24},{24,28},{1,5},{5,9},{9,... | collective-permute-start | bytes 393224 | tf_op jit(solution)/shard_map/ppermute | solution.py:16
  33.5 7.8 %collective-permute-start.2 = (f32[32,1,1024]{2,0,1:T(8,128)S(1)}, f32[32,1,1024]{2,0,1:T(8,128)S(1)}, u32[]{:S(2)}, u32[]{:S(2)}) collective-permute-start(f32[32,1,1024]{2,0,1:T(8,128)S(1)} %get-tuple-element.39), channel_id=1, source_target_pairs={{4,0},{8,4},{12,8},{16,12},{20,16},{24,20},{28,24},{5,1},{9,5},{13... | collective-permute-start | bytes 393224 | tf_op jit(solution)/shard_map/ppermute | solution.py:19
  34.8 9.4 %collective-permute-start.3 = (f32[32,1,1024]{2,0,1:T(8,128)S(1)}, f32[32,1,1024]{2,0,1:T(8,128)S(1)}, u32[]{:S(2)}, u32[]{:S(2)}) collective-permute-start(f32[32,1,1024]{2,0,1:T(8,128)S(1)} %get-tuple-element.38), channel_id=1, source_target_pairs={{0,4},{4,8},{8,12},{12,16},{16,20},{20,24},{24,28},{1,5},{5,9},{9,... | collective-permute-start | bytes 393224 | tf_op jit(solution)/shard_map/ppermute | solution.py:16
  44.9 7.8 %collective-permute-start.4 = (f32[32,1,1024]{2,0,1:T(8,128)S(1)}, f32[32,1,1024]{2,0,1:T(8,128)S(1)}, u32[]{:S(2)}, u32[]{:S(2)}) collective-permute-start(f32[32,1,1024]{2,0,1:T(8,128)S(1)} %get-tuple-element.35), channel_id=1, source_target_pairs={{4,0},{8,4},{12,8},{16,12},{20,16},{24,20},{28,24},{5,1},{9,5},{13... | collective-permute-start | bytes 393224 | tf_op jit(solution)/shard_map/ppermute | solution.py:19
  46.2 9.5 %collective-permute-start.5 = (f32[32,1,1024]{2,0,1:T(8,128)S(1)}, f32[32,1,1024]{2,0,1:T(8,128)S(1)}, u32[]{:S(2)}, u32[]{:S(2)}) collective-permute-start(f32[32,1,1024]{2,0,1:T(8,128)S(1)} %get-tuple-element.34), channel_id=1, source_target_pairs={{0,4},{4,8},{8,12},{12,16},{16,20},{20,24},{24,28},{1,5},{5,9},{9,... | collective-permute-start | bytes 393224 | tf_op jit(solution)/shard_map/ppermute | solution.py:16
  56.4 8.1 %collective-permute-start.6 = (f32[32,1,1024]{2,0,1:T(8,128)S(1)}, f32[32,1,1024]{2,0,1:T(8,128)S(1)}, u32[]{:S(2)}, u32[]{:S(2)}) collective-permute-start(f32[32,1,1024]{2,0,1:T(8,128)S(1)} %get-tuple-element.31), channel_id=1, source_target_pairs={{4,0},{8,4},{12,8},{16,12},{20,16},{24,20},{28,24},{5,1},{9,5},{13... | collective-permute-start | bytes 393224 | tf_op jit(solution)/shard_map/ppermute | solution.py:19
  57.7 9.7 %collective-permute-start.7 = (f32[32,1,1024]{2,0,1:T(8,128)S(1)}, f32[32,1,1024]{2,0,1:T(8,128)S(1)}, u32[]{:S(2)}, u32[]{:S(2)}) collective-permute-start(f32[32,1,1024]{2,0,1:T(8,128)S(1)} %get-tuple-element.30), channel_id=1, source_target_pairs={{0,4},{4,8},{8,12},{12,16},{16,20},{20,24},{24,28},{1,5},{5,9},{9,... | collective-permute-start | bytes 393224 | tf_op jit(solution)/shard_map/ppermute | solution.py:16
  68.1 8.1 %collective-permute-start.8 = (f32[32,1,1024]{2,0,1:T(8,128)S(1)}, f32[32,1,1024]{2,0,1:T(8,128)S(1)}, u32[]{:S(2)}, u32[]{:S(2)}) collective-permute-start(f32[32,1,1024]{2,0,1:T(8,128)S(1)} %get-tuple-element.27), channel_id=1, source_target_pairs={{4,0},{8,4},{12,8},{16,12},{20,16},{24,20},{28,24},{5,1},{9,5},{13... | collective-permute-start | bytes 393224 | tf_op jit(solution)/shard_map/ppermute | solution.py:19
  69.4 9.7 %collective-permute-start.9 = (f32[32,1,1024]{2,0,1:T(8,128)S(1)}, f32[32,1,1024]{2,0,1:T(8,128)S(1)}, u32[]{:S(2)}, u32[]{:S(2)}) collective-permute-start(f32[32,1,1024]{2,0,1:T(8,128)S(1)} %get-tuple-element.26), channel_id=1, source_target_pairs={{0,4},{4,8},{8,12},{12,16},{16,20},{20,24},{24,28},{1,5},{5,9},{9,... | collective-permute-start | bytes 393224 | tf_op jit(solution)/shard_map/ppermute | solution.py:16
  79.8 8.1 %collective-permute-start.10 = (f32[32,1,1024]{2,0,1:T(8,128)S(1)}, f32[32,1,1024]{2,0,1:T(8,128)S(1)}, u32[]{:S(2)}, u32[]{:S(2)}) collective-permute-start(f32[32,1,1024]{2,0,1:T(8,128)S(1)} %get-tuple-element.23), channel_id=1, source_target_pairs={{4,0},{8,4},{12,8},{16,12},{20,16},{24,20},{28,24},{5,1},{9,5},{13... | collective-permute-start | bytes 393224 | tf_op jit(solution)/shard_map/ppermute | solution.py:19
  81.1 9.7 %collective-permute-start.11 = (f32[32,1,1024]{2,0,1:T(8,128)S(1)}, f32[32,1,1024]{2,0,1:T(8,128)S(1)}, u32[]{:S(2)}, u32[]{:S(2)}) collective-permute-start(f32[32,1,1024]{2,0,1:T(8,128)S(1)} %get-tuple-element.22), channel_id=1, source_target_pairs={{0,4},{4,8},{8,12},{12,16},{16,20},{20,24},{24,28},{1,5},{5,9},{9,... | collective-permute-start | bytes 393224 | tf_op jit(solution)/shard_map/ppermute | solution.py:16
  91.5 8.1 %collective-permute-start.12 = (f32[32,1,1024]{2,0,1:T(8,128)S(1)}, f32[32,1,1024]{2,0,1:T(8,128)S(1)}, u32[]{:S(2)}, u32[]{:S(2)}) collective-permute-start(f32[32,1,1024]{2,0,1:T(8,128)S(1)} %get-tuple-element.19), channel_id=1, source_target_pairs={{4,0},{8,4},{12,8},{16,12},{20,16},{24,20},{28,24},{5,1},{9,5},{13... | collective-permute-start | bytes 393224 | tf_op jit(solution)/shard_map/ppermute | solution.py:19
  92.8 9.7 %collective-permute-start.13 = (f32[32,1,1024]{2,0,1:T(8,128)S(1)}, f32[32,1,1024]{2,0,1:T(8,128)S(1)}, u32[]{:S(2)}, u32[]{:S(2)}) collective-permute-start(f32[32,1,1024]{2,0,1:T(8,128)S(1)} %get-tuple-element.18), channel_id=1, source_target_pairs={{0,4},{4,8},{8,12},{12,16},{16,20},{20,24},{24,28},{1,5},{5,9},{9,... | collective-permute-start | bytes 393224 | tf_op jit(solution)/shard_map/ppermute | solution.py:16
  103.3 8.1 %collective-permute-start.14 = (f32[32,1,1024]{2,0,1:T(8,128)S(1)}, f32[32,1,1024]{2,0,1:T(8,128)S(1)}, u32[]{:S(2)}, u32[]{:S(2)}) collective-permute-start(f32[32,1,1024]{2,0,1:T(8,128)S(1)} %get-tuple-element.15), channel_id=1, source_target_pairs={{4,0},{8,4},{12,8},{16,12},{20,16},{24,20},{28,24},{5,1},{9,5},{13... | collective-permute-start | bytes 393224 | tf_op jit(solution)/shard_map/ppermute | solution.py:19
  104.6 9.7 %collective-permute-start.15 = (f32[32,1,1024]{2,0,1:T(8,128)S(1)}, f32[32,1,1024]{2,0,1:T(8,128)S(1)}, u32[]{:S(2)}, u32[]{:S(2)}) collective-permute-start(f32[32,1,1024]{2,0,1:T(8,128)S(1)} %get-tuple-element.14), channel_id=1, source_target_pairs={{0,4},{4,8},{8,12},{12,16},{16,20},{20,24},{24,28},{1,5},{5,9},{9,... | collective-permute-start | bytes 393224 | tf_op jit(solution)/shard_map/ppermute | solution.py:16
  114.3 10.4 %copy-start.4 = (f32[128]{0:T(128)S(1)}, f32[128]{0:T(128)}, u32[]{:S(2)}) copy-start(f32[128]{0:T(128)} %param.15) | copy-start | bytes 1540
  121.2 11.1 %all-to-all-start = ((f32[4,1,1024]{2,1,0:T(1,128)}), f32[4,1,1024]{2,1,0:T(1,128)S(1)}, u32[]{:S(2)}, u32[]{:S(2)}) async-start(f32[4,1,1024]{2,1,0:T(1,128)} %reshape.69), calls=%async_computation | async-start | bytes 32768 | tf_op jit(solution)/shard_map/all_to_all | solution.py:92
  127.4 42.8 %copy-start.6 = (f32[128]{0:T(128)S(1)}, f32[128]{0:T(128)}, u32[]{:S(2)}) copy-start(f32[128]{0:T(128)} %param.14) | copy-start | bytes 1540
  132.3 121.6 %all-to-all-start.1 = ((f32[4,1,65536]{2,1,0:T(1,128)}), f32[4,1,65536]{2,1,0:T(1,128)S(1)}, u32[]{:S(2)}, u32[]{:S(2)}) async-start(f32[4,1,65536]{2,1,0:T(1,128)} %reshape.67), calls=%async_computation.1 | async-start | bytes 2097152 | tf_op jit(solution)/shard_map/all_to_all | solution.py:116
  135.8 34.3 %all-reduce.19.cloned.1.call-start = ((), (), s32[]{:S(2)}) async-start(), calls=%async_computation.3 | async-start | bytes 131072 | tf_op jit(solution)/shard_map/psum | solution.py:97
  138.5 104.0 %all-reduce.21.cloned.1.call-start = ((), (), s32[]{:S(2)}) async-start(), calls=%async_computation.4 | async-start | bytes 131072 | tf_op jit(solution)/shard_map/psum | solution.py:97
Sparse Core Ops, SparseCore 0:
  139.0 31.1 all-reduce.18
  173.9 68.4 all-reduce.20
